TPU v7x, 32 devices: a whole 2x2x4 slice. The times are simulated.
32 devices in a mesh: dp: 8 (over z, x), mp: 4 (over y, core).
Axes of the slice: x: 2, y: 2, z: 4, core: 2. Of those that a mesh axis runs over, the one named last changes fastest.
Arguments:
- tokens: bfloat16 [8192, 2048], P(('dp', 'mp')), may hold values from -6 to 6
- cotangent: bfloat16 [8192, 2048], P(('dp', 'mp')), as said below
- gains_master: float32 [2, 2048], replicated, may hold values from 0.5 to 1.5
- scoring_master: float32 [2, 2048, 2048], P(None, 'dp', 'mp'), as said below
- mixing_master: float32 [2, 2048, 4096], P(None, 'dp', 'mp'), as said below
- output_master: float32 [4096, 2048], P(('mp', 'dp')), as said below
- expand_master: float32 [2048, 4096], P('dp', 'mp'), as said below
- shrink_master: float32 [4096, 2048], P(('mp', 'dp')), as said below
- gains_first: float32 [2, 2048], replicated, may hold values from -64 to 64
- gains_second: float32 [2, 2048], replicated, may hold values from 4.096 to 32.768
- scoring_first: float32 [2, 2048, 2048], P(None, 'dp', 'mp'), may hold values from -64 to 64
- scoring_second: float32 [2, 2048, 2048], P(None, 'dp', 'mp'), as said below
- mixing_first: float32 [2, 2048, 4096], P(None, 'dp', 'mp'), may hold values from -28 to 28
- mixing_second: float32 [2, 2048, 4096], P(None, 'dp', 'mp'), as said below
- output_first: float32 [4096, 2048], P(('mp', 'dp')), may hold values from -40 to 40
- output_second: float32 [4096, 2048], P(('mp', 'dp')), as said below
- expand_first: float32 [2048, 4096], P('dp', 'mp'), may hold values from -20 to 20
- expand_second: float32 [2048, 4096], P('dp', 'mp'), as said below
- shrink_first: float32 [4096, 2048], P(('mp', 'dp')), may hold values from -32 to 32
- shrink_second: float32 [4096, 2048], P(('mp', 'dp')), as said below
Outputs:
- layer_output: bfloat16 [8192, 2048], P(('dp', 'mp'))
- input_grad: float32 [8192, 2048], P(('dp', 'mp'))
- gains_grad: float32 [2, 2048], replicated
- scoring_grad: float32 [2, 2048, 2048], P(None, 'dp', 'mp')
- mixing_grad: float32 [2, 2048, 4096], P(None, 'dp', 'mp')
- output_grad: float32 [4096, 2048], P(('mp', 'dp'))
- expand_grad: float32 [2048, 4096], P('dp', 'mp')
- shrink_grad: float32 [4096, 2048], P(('mp', 'dp'))
- gains_moment: float32 [2, 2048], replicated
- scoring_moment: float32 [2, 2048, 2048], P(None, 'dp', 'mp')
- mixing_moment: float32 [2, 2048, 4096], P(None, 'dp', 'mp')
- output_moment: float32 [4096, 2048], P(('mp', 'dp'))
- expand_moment: float32 [2048, 4096], P('dp', 'mp')
- shrink_moment: float32 [4096, 2048], P(('mp', 'dp'))
- gains_square: float32 [2, 2048], replicated
- scoring_square: float32 [2, 2048, 2048], P(None, 'dp', 'mp')
- mixing_square: float32 [2, 2048, 4096], P(None, 'dp', 'mp')
- output_square: float32 [4096, 2048], P(('mp', 'dp'))
- expand_square: float32 [2048, 4096], P('dp', 'mp')
- shrink_square: float32 [4096, 2048], P(('mp', 'dp'))
- gains_weight: float32 [2, 2048], replicated
- scoring_weight: float32 [2, 2048, 2048], P(None, 'dp', 'mp')
- mixing_weight: float32 [2, 2048, 4096], P(None, 'dp', 'mp')
- output_weight: float32 [4096, 2048], P(('mp', 'dp'))
- expand_weight: float32 [2048, 4096], P('dp', 'mp')
- shrink_weight: float32 [4096, 2048], P(('mp', 'dp'))
- scoring_copy: bfloat16 [2, 2048, 2048], P(None, 'dp', 'mp')
- mixing_copy: bfloat16 [2, 2048, 4096], P(None, 'dp', 'mp')
- output_copy: bfloat16 [4096, 2048], P(('mp', 'dp'))
- expand_copy: bfloat16 [2048, 4096], P('dp', 'mp')
- shrink_copy: bfloat16 [4096, 2048], P(('mp', 'dp'))
- trust_norms: float32 [2, 9], replicated
Inputs may be any that keep to these rules, and one draw needn't show every extreme that they name: `cotangent`: entries of either sign. `scoring_master`: entries of either sign. `mixing_master`: entries of either sign. `output_master`: entries of either sign. `expand_master`: entries of either sign. `shrink_master`: entries of either sign. `scoring_second`: positive entries. `mixing_second`: positive entries. `output_second`: positive entries. `expand_second`: positive entries. `shrink_second`: positive entries.
All inputs are finite; a program needn't handle non-finite values.
Results may differ from a plain program's by a relative error of at most 0.017.
The roundings to bfloat16 on the way count: a program that leaves them out, or rounds other values in their place, can miss the bound.
Values may be sent and summed in bfloat16 or wider, within the bound.
A program may use at most 256 MiB of HBM per device.

v0:
```python
import jax
import jax.numpy as jnp
from jax import lax
from jax.sharding import PartitionSpec as P

DK = 256
DV = 512
beta_one = 0.9
beta_two = 0.999
lamb_epsilon = 1e-06
decay_rate = 0.01
learn_rate = 0.5
norm_epsilon = 1e-06


def rms_scale(values, gain_row):
    return (
        values
        * lax.rsqrt(jnp.mean(values * values, axis=-1, keepdims=True) + norm_epsilon)
        * gain_row
    )


def rotate(values, direction):
    length, heads, features = values.shape
    half = features // 2
    freqs = 10000.0 ** (-jnp.linspace(0.0, 1.0, half, dtype=jnp.float32))
    angle = jnp.arange(length, dtype=jnp.float32)[:, None] * freqs[None, :]
    cosine = jnp.cos(angle)[:, None, :]
    sine = direction * jnp.sin(angle)[:, None, :]
    pairs = values.reshape(length, heads, half, 2)
    even = pairs[..., 0]
    oddly = pairs[..., 1]
    turned = jnp.stack((even * cosine - oddly * sine, oddly * cosine + even * sine), axis=-1)
    return turned.reshape(length, heads, features)


def decay_table(offset, rows_count, length, decay_logs):
    row_pos = offset + jnp.arange(rows_count, dtype=jnp.int32)
    col_pos = jnp.arange(length, dtype=jnp.int32)
    spacing = (row_pos[:, None] - col_pos[None, :]).astype(jnp.float32)
    return jnp.where(
        spacing >= 0.0, jnp.exp(decay_logs[:, None, None] * jnp.maximum(spacing, 0.0)), 0.0
    )


def gate_norm(retained, gate_pre):
    normal = retained * lax.rsqrt(
        jnp.mean(retained * retained, axis=-1, keepdims=True) + norm_epsilon
    )
    return jax.nn.silu(gate_pre) * normal


def gelu_exact(values):
    return jax.nn.gelu(values, approximate=False)


def contract_rows(left, right):
    return lax.dot_general(
        left, right, (((0,), (0,)), ((), ())), preferred_element_type=jnp.float32
    )


def contract_cols(left, right):
    return lax.dot_general(
        left, right, (((1,), (1,)), ((), ())), preferred_element_type=jnp.float32
    )


def retention_forward(turned_queries, turned_keys, values, decay_logs, block_rows):
    length = turned_keys.shape[0]

    def one_block(block_index):
        offset = block_index * block_rows
        query_part = lax.dynamic_slice_in_dim(turned_queries, offset, block_rows, 0)
        scores = jnp.einsum(
            "qhd,khd->hqk", query_part, turned_keys, preferred_element_type=jnp.float32
        )
        weights = (scores * decay_table(offset, block_rows, length, decay_logs)).astype(
            jnp.bfloat16
        )
        retained = jnp.einsum("hqk,khe->qhe", weights, values, preferred_element_type=jnp.float32)
        return (retained, weights)

    retained_blocks, weight_blocks = lax.map(one_block, jnp.arange(length // block_rows))
    return (retained_blocks.reshape(length, values.shape[1], values.shape[2]), weight_blocks)


def retention_backward(turned_queries, turned_keys, values, retained_low, decay_logs, block_rows):
    length = turned_keys.shape[0]

    def one_block(totals, block_index):
        offset = block_index * block_rows
        query_part = lax.dynamic_slice_in_dim(turned_queries, offset, block_rows, 0)
        back_part = lax.dynamic_slice_in_dim(retained_low, offset, block_rows, 0)
        table = decay_table(offset, block_rows, length, decay_logs)
        scores = jnp.einsum(
            "qhd,khd->hqk", query_part, turned_keys, preferred_element_type=jnp.float32
        )
        weights = (scores * table).astype(jnp.bfloat16)
        weight_back = jnp.einsum(
            "qhe,khe->hqk", back_part, values, preferred_element_type=jnp.float32
        )
        score_back = (weight_back * table).astype(jnp.bfloat16)
        query_grad = jnp.einsum(
            "hqk,khd->qhd", score_back, turned_keys, preferred_element_type=jnp.float32
        )
        keys_total = totals[0] + jnp.einsum(
            "hqk,qhd->khd", score_back, query_part, preferred_element_type=jnp.float32
        )
        values_total = totals[1] + jnp.einsum(
            "hqk,qhe->khe", weights, back_part, preferred_element_type=jnp.float32
        )
        return ((keys_total, values_total), query_grad)

    start_totals = (jnp.zeros(turned_keys.shape, jnp.float32), jnp.zeros(values.shape, jnp.float32))
    (keys_grad, values_grad), query_blocks = lax.scan(
        one_block, start_totals, jnp.arange(length // block_rows)
    )
    return (query_blocks.reshape(turned_queries.shape), keys_grad, values_grad)


def lamb_parts(weight, grad, first, second):
    moment = beta_one * first + (1.0 - beta_one) * grad
    square = beta_two * second + (1.0 - beta_two) * grad * grad
    update = moment / (jnp.sqrt(square) + lamb_epsilon) + decay_rate * weight
    return (moment, square, update)


def body(
    tokens,
    cotangent,
    gains_master,
    scoring_master,
    mixing_master,
    output_master,
    expand_master,
    shrink_master,
    gains_first,
    gains_second,
    scoring_first,
    scoring_second,
    mixing_first,
    mixing_second,
    output_first,
    output_second,
    expand_first,
    expand_second,
    shrink_first,
    shrink_second,
):
    scoring_low, mixing_low, output_low, expand_low, shrink_low = (
        lax.all_gather(scoring_master.astype(jnp.bfloat16), "dp", axis=1, tiled=True),
        lax.all_gather(mixing_master.astype(jnp.bfloat16), "dp", axis=1, tiled=True),
        lax.all_gather(output_master.astype(jnp.bfloat16), "dp", axis=0, tiled=True),
        lax.all_gather(expand_master.astype(jnp.bfloat16), "dp", axis=0, tiled=True),
        lax.all_gather(shrink_master.astype(jnp.bfloat16), "dp", axis=0, tiled=True),
    )
    model_devices = lax.axis_size("mp")
    local_rows = tokens.shape[0]
    length = local_rows * model_devices
    heads_local = scoring_low.shape[2] // DK
    head_start = lax.axis_index("mp") * heads_local
    decay_logs = jnp.log(
        1.0
        - 2.0
        ** (-5.0 - (head_start + jnp.arange(heads_local, dtype=jnp.int32)).astype(jnp.float32))
    )
    block_rows = min(512, length)
    inputs = tokens.astype(jnp.float32)
    gain_one = gains_master[0]
    gain_two = gains_master[1]
    normed = rms_scale(inputs, gain_one).astype(jnp.bfloat16)
    normed_all = lax.all_gather(normed, "mp", axis=0, tiled=True)
    queries = jnp.dot(normed_all, scoring_low[0], preferred_element_type=jnp.float32)
    keys_pre = jnp.dot(normed_all, scoring_low[1], preferred_element_type=jnp.float32)
    values = (
        jnp.dot(normed_all, mixing_low[0], preferred_element_type=jnp.float32)
        .astype(jnp.bfloat16)
        .reshape(length, heads_local, DV)
    )
    gate_pre = jnp.dot(normed_all, mixing_low[1], preferred_element_type=jnp.float32).reshape(
        length, heads_local, DV
    )
    turned_queries = rotate(queries.reshape(length, heads_local, DK), 1.0).astype(jnp.bfloat16)
    turned_keys = rotate(keys_pre.reshape(length, heads_local, DK), 1.0).astype(jnp.bfloat16)
    retained, weight_blocks = retention_forward(
        turned_queries, turned_keys, values, decay_logs, block_rows
    )
    mixed_rows = (
        gate_norm(retained, gate_pre).reshape(length, heads_local * DV).astype(jnp.bfloat16)
    )
    branch = lax.psum_scatter(
        jnp.dot(mixed_rows, output_low, preferred_element_type=jnp.float32),
        "mp",
        scatter_dimension=0,
        tiled=True,
    )
    hidden = inputs + branch
    second_in = rms_scale(hidden, gain_two).astype(jnp.bfloat16)
    second_all = lax.all_gather(second_in, "mp", axis=0, tiled=True)
    upward = jnp.dot(second_all, expand_low, preferred_element_type=jnp.float32)
    active = gelu_exact(upward).astype(jnp.bfloat16)
    ffn_branch = lax.psum_scatter(
        jnp.dot(active, shrink_low, preferred_element_type=jnp.float32),
        "mp",
        scatter_dimension=0,
        tiled=True,
    )
    layer_output = (hidden + ffn_branch).astype(jnp.bfloat16)
    back_all = lax.all_gather(cotangent, "mp", axis=0, tiled=True)
    shrink_local = contract_rows(active, back_all)
    active_back = contract_cols(back_all, shrink_low)
    gelu_pull = jax.vjp(gelu_exact, upward)[1]
    upward_back = gelu_pull(active_back)[0].astype(jnp.bfloat16)
    expand_local = contract_rows(second_all, upward_back)
    second_back = lax.psum_scatter(
        contract_cols(upward_back, expand_low), "mp", scatter_dimension=0, tiled=True
    )
    norm_two_pull = jax.vjp(rms_scale, hidden, gain_two)[1]
    hidden_part, gain_two_grad = norm_two_pull(second_back)
    hidden_back = cotangent.astype(jnp.float32) + hidden_part
    branch_back = hidden_back.astype(jnp.bfloat16)
    branch_all = lax.all_gather(branch_back, "mp", axis=0, tiled=True)
    output_local = contract_rows(mixed_rows, branch_all)
    mixed_back = contract_cols(branch_all, output_low)
    gate_pull = jax.vjp(gate_norm, retained, gate_pre)[1]
    retained_back, gate_back = gate_pull(mixed_back.reshape(length, heads_local, DV))
    retained_low = retained_back.astype(jnp.bfloat16)
    gate_low = gate_back.astype(jnp.bfloat16).reshape(length, heads_local * DV)
    turned_query_back, turned_key_back, values_back = retention_backward(
        turned_queries, turned_keys, values, retained_low, decay_logs, block_rows
    )
    query_low = (
        rotate(turned_query_back, -1.0).astype(jnp.bfloat16).reshape(length, heads_local * DK)
    )
    keys_low = rotate(turned_key_back, -1.0).astype(jnp.bfloat16).reshape(length, heads_local * DK)
    values_low = values_back.astype(jnp.bfloat16).reshape(length, heads_local * DV)
    scoring_local = jnp.stack(
        (contract_rows(normed_all, query_low), contract_rows(normed_all, keys_low))
    )
    mixing_local = jnp.stack(
        (contract_rows(normed_all, values_low), contract_rows(normed_all, gate_low))
    )
    total = contract_cols(query_low, scoring_low[0])
    total = total + contract_cols(keys_low, scoring_low[1])
    total = total + contract_cols(values_low, mixing_low[0])
    normed_back = lax.psum_scatter(
        total + contract_cols(gate_low, mixing_low[1]), "mp", scatter_dimension=0, tiled=True
    )
    norm_one_pull = jax.vjp(rms_scale, inputs, gain_one)[1]
    inputs_part, gain_one_grad = norm_one_pull(normed_back)
    input_grad = hidden_back + inputs_part
    scoring_grad, mixing_grad, output_grad, expand_grad, shrink_grad = (
        lax.psum_scatter(scoring_local, "dp", scatter_dimension=1, tiled=True),
        lax.psum_scatter(mixing_local, "dp", scatter_dimension=1, tiled=True),
        lax.psum_scatter(output_local, "dp", scatter_dimension=0, tiled=True),
        lax.psum_scatter(expand_local, "dp", scatter_dimension=0, tiled=True),
        lax.psum_scatter(shrink_local, "dp", scatter_dimension=0, tiled=True),
    )
    gains_grad = lax.psum(jnp.stack((gain_one_grad, gain_two_grad)), ("dp", "mp"))
    scoring_moment, scoring_square, scoring_update = lamb_parts(
        scoring_master, scoring_grad, scoring_first, scoring_second
    )
    mixing_moment, mixing_square, mixing_update = lamb_parts(
        mixing_master, mixing_grad, mixing_first, mixing_second
    )
    output_moment, output_square, output_update = lamb_parts(
        output_master, output_grad, output_first, output_second
    )
    expand_moment, expand_square, expand_update = lamb_parts(
        expand_master, expand_grad, expand_first, expand_second
    )
    shrink_moment, shrink_square, shrink_update = lamb_parts(
        shrink_master, shrink_grad, shrink_first, shrink_second
    )
    gains_moment, gains_square, gains_update = lamb_parts(
        gains_master, gains_grad, gains_first, gains_second
    )
    weight_local = jnp.concatenate(
        (
            jnp.sum(scoring_master * scoring_master, axis=(1, 2)),
            jnp.sum(mixing_master * mixing_master, axis=(1, 2)),
            jnp.stack(
                (
                    jnp.sum(output_master * output_master),
                    jnp.sum(expand_master * expand_master),
                    jnp.sum(shrink_master * shrink_master),
                )
            ),
        )
    )
    update_local = jnp.concatenate(
        (
            jnp.sum(scoring_update * scoring_update, axis=(1, 2)),
            jnp.sum(mixing_update * mixing_update, axis=(1, 2)),
            jnp.stack(
                (
                    jnp.sum(output_update * output_update),
                    jnp.sum(expand_update * expand_update),
                    jnp.sum(shrink_update * shrink_update),
                )
            ),
        )
    )
    weight_total, update_total = lax.psum((weight_local, update_local), ("dp", "mp"))
    weight_norms = jnp.sqrt(weight_total)
    update_norms = jnp.sqrt(update_total)
    ratios = weight_norms / update_norms
    gains_wnorm = jnp.sqrt(jnp.sum(gains_master * gains_master, axis=1))
    gains_unorm = jnp.sqrt(jnp.sum(gains_update * gains_update, axis=1))
    scoring_weight = scoring_master - learn_rate * ratios[0:2][:, None, None] * scoring_update
    mixing_weight = mixing_master - learn_rate * ratios[2:4][:, None, None] * mixing_update
    output_weight = output_master - learn_rate * ratios[4] * output_update
    expand_weight = expand_master - learn_rate * ratios[5] * expand_update
    shrink_weight = shrink_master - learn_rate * ratios[6] * shrink_update
    gains_weight = gains_master - learn_rate * (gains_wnorm / gains_unorm)[:, None] * gains_update
    trust_norms = jnp.stack(
        (jnp.concatenate((weight_norms, gains_wnorm)), jnp.concatenate((update_norms, gains_unorm)))
    )
    return (
        layer_output,
        input_grad,
        gains_grad,
        scoring_grad,
        mixing_grad,
        output_grad,
        expand_grad,
        shrink_grad,
        gains_moment,
        scoring_moment,
        mixing_moment,
        output_moment,
        expand_moment,
        shrink_moment,
        gains_square,
        scoring_square,
        mixing_square,
        output_square,
        expand_square,
        shrink_square,
        gains_weight,
        scoring_weight,
        mixing_weight,
        output_weight,
        expand_weight,
        shrink_weight,
        scoring_weight.astype(jnp.bfloat16),
        mixing_weight.astype(jnp.bfloat16),
        output_weight.astype(jnp.bfloat16),
        expand_weight.astype(jnp.bfloat16),
        shrink_weight.astype(jnp.bfloat16),
        trust_norms,
    )


def solution(mesh):
    placed = (
        P(("dp", "mp"), None),
        P(("dp", "mp"), None),
        P(),
        P(None, "dp", "mp"),
        P(None, "dp", "mp"),
        P(("mp", "dp"), None),
        P("dp", "mp"),
        P(("mp", "dp"), None),
        P(),
        P(),
        P(None, "dp", "mp"),
        P(None, "dp", "mp"),
        P(None, "dp", "mp"),
        P(None, "dp", "mp"),
        P(("mp", "dp"), None),
        P(("mp", "dp"), None),
        P("dp", "mp"),
        P("dp", "mp"),
        P(("mp", "dp"), None),
        P(("mp", "dp"), None),
    )
    return jax.shard_map(
        body,
        mesh=mesh,
        in_specs=placed,
        out_specs=(
            P(("dp", "mp"), None),
            P(("dp", "mp"), None),
            P(),
            P(None, "dp", "mp"),
            P(None, "dp", "mp"),
            P(("mp", "dp"), None),
            P("dp", "mp"),
            P(("mp", "dp"), None),
            P(),
            P(None, "dp", "mp"),
            P(None, "dp", "mp"),
            P(("mp", "dp"), None),
            P("dp", "mp"),
            P(("mp", "dp"), None),
            P(),
            P(None, "dp", "mp"),
            P(None, "dp", "mp"),
            P(("mp", "dp"), None),
            P("dp", "mp"),
            P(("mp", "dp"), None),
            P(),
            P(None, "dp", "mp"),
            P(None, "dp", "mp"),
            P(("mp", "dp"), None),
            P("dp", "mp"),
            P(("mp", "dp"), None),
            P(None, "dp", "mp"),
            P(None, "dp", "mp"),
            P(("mp", "dp"), None),
            P("dp", "mp"),
            P(("mp", "dp"), None),
            P(),
        ),
        check_vma=False,
    )
```

profile of v0, /device:TPU:0, one launch (start us, length us, event | category | flops | bytes accessed | tf_op | source)
XLA Modules:
  0.0 1868.9 jit_solution(18121619089342116246)
XLA Ops:
  21.0 65.3 %all-gather.14.cloned.1.call-done = bf16[2,2048,512]{2,1,0:T(8,128)(2,1)} async-done(((bf16[2,256,512]{2,1,0:T(8,128)(2,1)}), bf16[2,2048,512]{2,1,0:T(8,128)(2,1)}) %all-gather.14.cloned.1.call-update) | async-done | bytes 4194320 | tf_op jit(solution)/shard_map/all_gather | solution.py:153
  86.3 4.5 slice_bitcast_fusion.6
  102.0 19.4 %all-gather.10.cloned.1.call-done = bf16[1024,2048]{1,0:T(8,128)(2,1)} async-done(((bf16[256,2048]{1,0:T(8,128)(2,1)}), bf16[1024,2048]{1,0:T(8,128)(2,1)}) %all-gather.10.cloned.1.call-update) | async-done | bytes 4194320 | tf_op jit(solution)/shard_map/all_gather | solution.py:174
  121.5 5.4 fusion.20
  135.9 112.8 %all-gather.12.cloned.1.call-done = bf16[2,2048,1024]{2,1,0:T(8,128)(2,1)} async-done(((bf16[2,256,1024]{2,1,0:T(8,128)(2,1)}), bf16[2,2048,1024]{2,1,0:T(8,128)(2,1)}) %all-gather.12.cloned.1.call-update) | async-done | bytes 8388624 | tf_op jit(solution)/shard_map/all_gather | solution.py:154
  248.7 8.0 fusion.51
  259.3 4.7 slice_bitcast_fusion.3
  264.0 6.5 copy.86
  270.5 18.0 while.26
  273.9 5.4 bitcast_dynamic-update-slice_fusion.2
  282.8 5.7 bitcast_dynamic-update-slice_fusion.2
  288.5 7.3 copy.96
  295.8 7.0 reshape.309
  306.3 10.5 multiply_convert_fusion.4
  316.8 5.5 all-gather.16.cloned.1.call-done
  322.3 8.9 fusion.83
  333.4 68.0 %reduce-scatter.10.cloned.1.call-done = f32[256,2048]{1,0:T(8,128)} async-done(((f32[1024,2048]{1,0:T(8,128)}), f32[256,2048]{1,0:T(8,128)}) %reduce-scatter.10.cloned.1.call-update) | async-done | bytes 2097168 | tf_op jit(solution)/shard_map/reduce_scatter | solution.py:193
  407.8 68.9 %all-gather.20.cloned.1.call-done = bf16[2048,1024]{1,0:T(8,128)(2,1)} async-done(((bf16[256,1024]{1,0:T(8,128)(2,1)}), bf16[2048,1024]{1,0:T(8,128)(2,1)}) %all-gather.20.cloned.1.call-update) | async-done | bytes 4194320 | tf_op jit(solution)/shard_map/all_gather | solution.py:156
  476.7 35.2 %all-gather.18.cloned.1.call-done = bf16[1024,2048]{1,0:T(8,128)(2,1)} async-done(((bf16[256,2048]{1,0:T(8,128)(2,1)}), bf16[1024,2048]{1,0:T(8,128)(2,1)}) %all-gather.18.cloned.1.call-update) | async-done | bytes 4194320 | tf_op jit(solution)/shard_map/all_gather | solution.py:201
  511.9 9.9 fusion.84
  521.8 26.1 %all-gather.24.cloned.1.call-done = bf16[1024,2048]{1,0:T(8,128)(2,1)} async-done(((bf16[256,2048]{1,0:T(8,128)(2,1)}), bf16[1024,2048]{1,0:T(8,128)(2,1)}) %all-gather.24.cloned.1.call-update) | async-done | bytes 4194320 | tf_op jit(solution)/shard_map/all_gather | solution.py:211
  547.9 75.5 %all-gather.22.cloned.1.call-done = bf16[1024,2048]{1,0:T(8,128)(2,1)} async-done(((bf16[128,2048]{1,0:T(8,128)(2,1)}), bf16[1024,2048]{1,0:T(8,128)(2,1)}) %all-gather.22.cloned.1.call-update) | async-done | bytes 4194320 | tf_op jit(solution)/shard_map/all_gather | solution.py:157
  623.5 18.9 %add_convert_fusion = (bf16[1024,1024]{1,0:T(8,128)(2,1)S(1)}, f32[1024,1024]{1,0:T(8,128)}) fusion(f32[1024,1024]{1,0:T(8,128)} %fusion.84, bf16[1024,2048]{1,0:T(8,128)(2,1)} %all-gather.24.cloned.1.call-done, bf16[1024,2048]{1,0:T(8,128)(2,1)} %all-gather.22.cloned.1.call-done), kind=kOutput, calls=%fused_computation.54 | convolution fusion | flops 4370464768 | bytes 18874368 | tf_op jit(solution)/shard_map/dot_general | solution.py:65
  643.6 6.8 fusion.86
  650.5 70.1 %reduce-scatter.14.cloned.1.call-done = f32[256,2048]{1,0:T(8,128)} async-done(((f32[1024,2048]{1,0:T(8,128)}), f32[256,2048]{1,0:T(8,128)}) %reduce-scatter.14.cloned.1.call-update) | async-done | bytes 2097168 | tf_op jit(solution)/shard_map/reduce_scatter | solution.py:217
  725.8 4.7 multiply_convert_fusion.3
  731.9 7.1 fusion.89
  740.7 9.0 fusion.88
  749.8 10.6 all-gather.26.cloned.1.call-done
  760.4 11.1 multiply_reduce_fusion
  771.6 4.5 fusion.16
  776.0 81.4 %while.27 = (s32[]{:T(128)}, f32[1024,2,256]{0,2,1:T(8,128)}, f32[1024,2,512]{0,2,1:T(8,128)}, f32[2,512,2,256]{1,0,3,2:T(2,128)}, s32[2]{0:T(128)S(1)}, /*index...) while((s32[]{:T(128)}, f32[1024,2,256]{0,2,1:T(8,128)}, ...), condition=%wide.region_11.13_spmd.clone, body=%wide.region_10.12_spmd.clone.sunk | while | flops 3772776960 | bytes 48765212 | solution.py:117
  779.5 4.6 multiply_convert_fusion.7
  788.9 6.8 bitcast_add_fusion.5
  795.7 19.6 %dynamic_update_slice.14 = f32[2,512,2,256]{1,0,3,2:T(2,128)} dynamic-update-slice(f32[2,512,2,256]{1,0,3,2:T(2,128)} %get-tuple-element.510, f32[1,512,2,256]{1,0,3,2:T(1,128)S(1)} %copy.168, s32[]{:T(128)S(6)} %copy.181, s32[]{:T(128)} %constant.79.clone.1..sunk.1, s32[]{:T(128)} %constant.79.clone.1..sunk.1, s32[]{:T(128)} %constant.79.clone.1..sunk.1) | dynamic-update-slice | bytes 2097156 | tf_op jit(solution)/shard_map/while/body/jit(dynamic_update_index_in_dim)/dynamic_update_slice | solution.py:117
  818.8 4.6 multiply_convert_fusion.7
  825.4 3.7 bitcast_add_fusion.4
  829.8 8.0 bitcast_add_fusion.5
  837.8 19.6 %dynamic_update_slice.14 = f32[2,512,2,256]{1,0,3,2:T(2,128)} dynamic-update-slice(f32[2,512,2,256]{1,0,3,2:T(2,128)} %get-tuple-element.510, f32[1,512,2,256]{1,0,3,2:T(1,128)S(1)} %copy.168, s32[]{:T(128)S(6)} %copy.181, s32[]{:T(128)} %constant.79.clone.1..sunk.1, s32[]{:T(128)} %constant.79.clone.1..sunk.1, s32[]{:T(128)} %constant.79.clone.1..sunk.1) | dynamic-update-slice | bytes 2097156 | tf_op jit(solution)/shard_map/while/body/jit(dynamic_update_index_in_dim)/dynamic_update_slice | solution.py:117
  857.4 4.0 reshape_reshape.2
  861.5 3.2 copy.105
  878.3 9.8 fusion.24
  888.1 6.9 fusion.34
  895.0 12.3 add_add_fusion
  907.3 10.6 fusion.87
  918.2 4.8 convolution_bitcast_fusion.4
  925.4 4.3 pad_maximum_fusion.1
  931.3 8.9 fusion.85
  940.3 7.2 convolution_bitcast_fusion.2
  947.6 4.7 convolution_bitcast_fusion.1
  952.3 6.4 pad_maximum_fusion
  960.2 4.5 multiply_reduce_fusion.11
  964.7 98.1 %reduce-scatter.24.cloned.1.call-done = f32[256,1024]{1,0:T(8,128)} async-done(((f32[2048,1024]{1,0:T(8,128)}), f32[256,1024]{1,0:T(8,128)}) %reduce-scatter.24.cloned.1.call-update) | async-done | bytes 1048592 | tf_op jit(solution)/shard_map/reduce_scatter | solution.py:258
  1062.8 4.5 multiply_reduce_fusion.12
  1067.3 68.4 %reduce-scatter.16.cloned.1.call-done = f32[256,2048]{1,0:T(8,128)} async-done(((f32[1024,2048]{1,0:T(8,128)}), f32[256,2048]{1,0:T(8,128)}) %reduce-scatter.16.cloned.1.call-update) | async-done | bytes 2097168 | tf_op jit(solution)/shard_map/reduce_scatter | solution.py:248
  1138.1 149.2 %reduce-scatter.22.cloned.1.call-done = f32[128,2048]{1,0:T(8,128)} async-done(((f32[1024,2048]{1,0:T(8,128)}), f32[128,2048]{1,0:T(8,128)}) %reduce-scatter.22.cloned.1.call-update) | async-done | bytes 1048592 | tf_op jit(solution)/shard_map/reduce_scatter | solution.py:257
  1287.2 4.5 multiply_reduce_fusion.13
  1291.8 146.1 %reduce-scatter.18.cloned.1.call-done = f32[2,256,512]{2,1,0:T(8,128)} async-done(((f32[2,2048,512]{2,1,0:T(8,128)}), f32[2,256,512]{2,1,0:T(8,128)}) %reduce-scatter.18.cloned.1.call-update) | async-done | bytes 1048592 | tf_op jit(solution)/shard_map/reduce_scatter | solution.py:255
  1437.9 4.3 multiply_reduce_fusion.14
  1442.2 68.7 %reduce-scatter.12.cloned.1.call-done = f32[256,2048]{1,0:T(8,128)} async-done(((f32[1024,2048]{1,0:T(8,128)}), f32[256,2048]{1,0:T(8,128)}) %reduce-scatter.12.cloned.1.call-update) | async-done | bytes 2097168 | tf_op jit(solution)/shard_map/reduce_scatter | solution.py:204
  1510.9 5.9 fusion.42
  1516.9 277.7 %reduce-scatter.20.cloned.1.call-done = f32[2,256,1024]{2,1,0:T(8,128)} async-done(((f32[2,2048,1024]{2,1,0:T(8,128)}), f32[2,256,1024]{2,1,0:T(8,128)}) %reduce-scatter.20.cloned.1.call-update) | async-done | bytes 2097168 | tf_op jit(solution)/shard_map/reduce_scatter | solution.py:256
  1794.6 7.1 multiply_reduce_fusion.3
  1805.9 39.4 %all-reduce = (f32[2,2048]{1,0:T(2,128)S(1)}, f32[7]{0:T(128)S(1)}, f32[7]{0:T(128)S(1)}) all-reduce(f32[2,2048]{1,0:T(2,128)S(1)} %pad_maximum_fusion.4, f32[7]{0:T(128)S(1)} %concatenate.16, f32[7]{0:T(128)S(1)} %concatenate.15), channel_id=1, replica_groups=mesh['dp'=8,'mp'=4] {'dp','mp'}, use_global_device_ids=true, to_apply=%region_16.18 | all-reduce | flops 4110 | bytes 32880 | tf_op jit(solution)/shard_map/psum | solution.py:261
  (275 shorter events, 116.5 us)
Async XLA Ops:
  7.2 8.5 copy-start.5
  7.2 79.1 %all-gather.14.cloned.1.call-start = ((), (), s32[]{:S(2)}) async-start(), calls=%async_computation.11 | async-start | bytes 4718592 | tf_op jit(solution)/shard_map/all_gather | solution.py:153
  9.5 7.4 copy-start.17
  9.5 112.0 %all-gather.10.cloned.1.call-start = ((), (), s32[]{:S(2)}) async-start(), calls=%async_computation.9 | async-start | bytes 5242880 | tf_op jit(solution)/shard_map/all_gather | solution.py:174
  12.6 710.9 %copy-start.41 = (f32[1,2048]{1,0:T(1,128)}, f32[1,2048]{1,0:T(1,128)S(1)}, u32[]{:S(2)}) copy-start(f32[1,2048]{1,0:T(1,128)S(1)} %get-tuple-element.334) | copy-start | bytes 24580
  15.7 233.1 %all-gather.12.cloned.1.call-start = ((), (), s32[]{:S(2)}) async-start(), calls=%async_computation.10 | async-start | bytes 9437184 | tf_op jit(solution)/shard_map/all_gather | solution.py:154
  16.9 305.4 %all-gather.16.cloned.1.call-start = ((), (), s32[]{:S(2)}) async-start(), calls=%async_computation.12 | async-start | bytes 4718592 | tf_op jit(solution)/shard_map/all_gather | solution.py:155
  17.8 383.5 %reduce-scatter.10.cloned.1.call-start = ((), (), s32[]{:S(2)}) async-start(), calls=%async_computation.13 | async-start | bytes 10485760 | tf_op jit(solution)/shard_map/reduce_scatter | solution.py:193
  21.0 108.5 %copy-start.23 = (f32[1024,128]{0,1:T(8,128)}, f32[1024,128]{0,1:T(8,128)S(1)}, u32[]{:S(2)}) copy-start(f32[1024,128]{0,1:T(8,128)S(1)} %get-tuple-element.349) | copy-start | bytes 1572868
  102.0 24.9 %copy-start.39 = (bf16[2,128,2,2048]{3,2,1,0:T(2,128)(2,1)S(1)}, bf16[2,128,2,2048]{3,2,1,0:T(2,128)(2,1)}, u32[]{:S(2)}) copy-start(bf16[2,128,2,2048]{3,2,1,0:T(2,128)(2,1)} %dot_general.100) | copy-start | bytes 6291460
  121.5 5.4 copy-start.58
  316.8 14.4 copy-start.63
  331.2 70.1 %copy-start.3 = (bf16[256,2048]{1,0:T(8,128)(2,1)S(1)}, bf16[256,2048]{1,0:T(8,128)(2,1)}, u32[]{:S(2)}) copy-start(bf16[256,2048]{1,0:T(8,128)(2,1)} %param.26) | copy-start | bytes 3145732
  331.2 145.5 %all-gather.20.cloned.1.call-start = ((), (), s32[]{:S(2)}) async-start(), calls=%async_computation.15 | async-start | bytes 4718592 | tf_op jit(solution)/shard_map/all_gather | solution.py:156
  333.3 178.5 %all-gather.18.cloned.1.call-start = ((), (), s32[]{:S(2)}) async-start(), calls=%async_computation.14 | async-start | bytes 5242880 | tf_op jit(solution)/shard_map/all_gather | solution.py:201
  403.3 320.2 %copy-start = (f32[256,2048]{1,0:T(8,128)}, f32[256,2048]{1,0:T(8,128)S(1)}, u32[]{:S(2)}) copy-start(f32[256,2048]{1,0:T(8,128)S(1)} %get-tuple-element.310) | copy-start | bytes 6291460
  403.3 320.2 %copy-start.47 = (f32[256]{0:T(256)}, f32[256]{0:T(256)S(1)}, u32[]{:S(2)}) copy-start(f32[256]{0:T(256)S(1)} %fusion.62) | copy-start | bytes 3076
  404.8 143.1 %all-gather.24.cloned.1.call-start = ((), (), s32[]{:S(2)}) async-start(), calls=%async_computation.18 | async-start | bytes 5242880 | tf_op jit(solution)/shard_map/all_gather | solution.py:211
  405.6 217.9 %all-gather.22.cloned.1.call-start = ((), (), s32[]{:S(2)}) async-start(), calls=%async_computation.16 | async-start | bytes 4718592 | tf_op jit(solution)/shard_map/all_gather | solution.py:157
  407.7 312.9 %reduce-scatter.14.cloned.1.call-start = ((), (), s32[]{:S(2)}) async-start(), calls=%async_computation.19 | async-start | bytes 10485760 | tf_op jit(solution)/shard_map/reduce_scatter | solution.py:217
  623.4 20.2 %copy-start.62 = (bf16[2048,1024]{1,0:T(8,128)(2,1)S(1)}, bf16[2048,1024]{1,0:T(8,128)(2,1)}, u32[]{:S(2)}) copy-start(bf16[2048,1024]{1,0:T(8,128)(2,1)} %all-gather.20.cloned.1.call-done) | copy-start | bytes 12582916
  650.5 73.6 %copy-start.11 = (bf16[256,2048]{1,0:T(8,128)(2,1)S(1)}, bf16[256,2048]{1,0:T(8,128)(2,1)}, u32[]{:S(2)}) copy-start(bf16[256,2048]{1,0:T(8,128)(2,1)} %param.27) | copy-start | bytes 3145732
  650.5 109.9 %all-gather.26.cloned.1.call-start = ((), (), s32[]{:S(2)}) async-start(), calls=%async_computation.20 | async-start | bytes 5242880 | tf_op jit(solution)/shard_map/all_gather | solution.py:224
  725.8 232.9 %reduce-scatter.26.cloned.1.call-start = ((), (), s32[]{:S(2)}) async-start(), calls=%async_computation.26 | async-start | bytes 9437184 | tf_op jit(solution)/shard_map/reduce_scatter | solution.py:259
  725.8 6.1 copy-start.61
  739.1 323.7 %reduce-scatter.24.cloned.1.call-start = ((), (), s32[]{:S(2)}) async-start(), calls=%async_computation.25 | async-start | bytes 9437184 | tf_op jit(solution)/shard_map/reduce_scatter | solution.py:258
  749.7 386.0 %reduce-scatter.16.cloned.1.call-start = ((), (), s32[]{:S(2)}) async-start(), calls=%async_computation.21 | async-start | bytes 10485760 | tf_op jit(solution)/shard_map/reduce_scatter | solution.py:248
  760.4 11.2 copy-start.9
  760.4 11.2 copy-start.25
  779.5 4.6 copy-start.2
  818.8 4.6 copy-start.2
  875.9 12.2 copy-start.38
  875.9 12.2 slice-start
  878.3 9.8 slice-start.1
  907.3 380.0 %reduce-scatter.22.cloned.1.call-start = ((), (), s32[]{:S(2)}) async-start(), calls=%async_computation.24 | async-start | bytes 9437184 | tf_op jit(solution)/shard_map/reduce_scatter | solution.py:257
  917.9 520.0 %reduce-scatter.18.cloned.1.call-start = ((), (), s32[]{:S(2)}) async-start(), calls=%async_computation.22 | async-start | bytes 9437184 | tf_op jit(solution)/shard_map/reduce_scatter | solution.py:255
  918.2 4.8 copy-start.59
  929.7 581.2 %reduce-scatter.12.cloned.1.call-start = ((), (), s32[]{:S(2)}) async-start(), calls=%async_computation.17 | async-start | bytes 10485760 | tf_op jit(solution)/shard_map/reduce_scatter | solution.py:204
  940.2 7.3 copy-start.37
  940.3 854.4 %reduce-scatter.20.cloned.1.call-start = ((), (), s32[]{:S(2)}) async-start(), calls=%async_computation.23 | async-start | bytes 18874368 | tf_op jit(solution)/shard_map/reduce_scatter | solution.py:256
  940.3 7.3 copy-start.60
  958.7 104.1 %copy-start.15 = (f32[256,1024]{1,0:T(8,128)S(1)}, f32[256,1024]{1,0:T(8,128)}, u32[]{:S(2)}) copy-start(f32[256,1024]{1,0:T(8,128)} %param.32) | copy-start | bytes 3145732
  964.6 171.1 %copy-start.4 = (bf16[256,2048]{1,0:T(8,128)(2,1)S(1)}, bf16[256,2048]{1,0:T(8,128)(2,1)}, u32[]{:S(2)}) copy-start(bf16[256,2048]{1,0:T(8,128)(2,1)} %param.26) | copy-start | bytes 3145732
  964.6 171.1 %copy-start.45 = (f32[1,2048]{1,0:T(1,128)S(1)}, f32[1,2048]{1,0:T(1,128)}, u32[]{:S(2)}) copy-start(f32[1,2048]{1,0:T(1,128)} %copy-done.44) | copy-start | bytes 24580
  964.6 171.1 %copy-start.50 = (f32[256]{0:T(256)S(1)}, f32[256]{0:T(256)}, u32[]{:S(2)}) copy-start(f32[256]{0:T(256)} %copy-done.49) | copy-start | bytes 3076
  964.6 173.4 %copy-start.57 = (f32[256]{0:T(256)S(1)}, f32[256]{0:T(256)}, u32[]{:S(2)}) copy-start(f32[256]{0:T(256)} %copy-done.56) | copy-start | bytes 3076
  964.6 173.4 %copy-start.46 = (f32[2048]{0:T(1024)S(1)}, f32[2048]{0:T(1024)}, u32[]{:S(2)}) copy-start(f32[2048]{0:T(1024)} %get-tuple-element.232) | copy-start | bytes 24580
  964.7 322.6 %copy-start.18 = (f32[128,2048]{1,0:T(8,128)S(1)}, f32[128,2048]{1,0:T(8,128)}, u32[]{:S(2)}) copy-start(f32[128,2048]{1,0:T(8,128)} %param.31) | copy-start | bytes 3145732
  1291.8 219.1 %copy-start.1 = (f32[256,2048]{1,0:T(8,128)S(1)}, f32[256,2048]{1,0:T(8,128)}, u32[]{:S(2)}) copy-start(f32[256,2048]{1,0:T(8,128)} %copy-done) | copy-start | bytes 6291460
  1291.8 219.1 %copy-start.42 = (f32[1,2048]{1,0:T(1,128)S(1)}, f32[1,2048]{1,0:T(1,128)}, u32[]{:S(2)}) copy-start(f32[1,2048]{1,0:T(1,128)} %copy-done.41) | copy-start | bytes 24580
  1291.8 219.1 %copy-start.48 = (f32[256]{0:T(256)S(1)}, f32[256]{0:T(256)}, u32[]{:S(2)}) copy-start(f32[256]{0:T(256)} %copy-done.47) | copy-start | bytes 3076
  1291.8 219.1 %copy-start.55 = (f32[256]{0:T(256)S(1)}, f32[256]{0:T(256)}, u32[]{:S(2)}) copy-start(f32[256]{0:T(256)} %copy-done.54) | copy-start | bytes 3076
  1516.8 331.1 %copy-start.43 = (f32[2,2048]{1,0:T(2,128)S(1)}, f32[2,2048]{1,0:T(2,128)}, u32[]{:S(2)}) copy-start(f32[2,2048]{1,0:T(2,128)} %param.28) | copy-start | bytes 49156
  1516.8 331.1 %copy-start.51 = (f32[2,2048]{1,0:T(2,128)S(1)}, f32[2,2048]{1,0:T(2,128)}, u32[]{:S(2)}) copy-start(f32[2,2048]{1,0:T(2,128)} %param.35) | copy-start | bytes 49156
  1516.8 331.1 %copy-start.52 = (f32[2,2048]{1,0:T(2,128)S(1)}, f32[2,2048]{1,0:T(2,128)}, u32[]{:S(2)}) copy-start(f32[2,2048]{1,0:T(2,128)} %param.34) | copy-start | bytes 49156
  1516.8 333.4 %copy-start.13 = (f32[128,2048]{1,0:T(8,128)S(1)}, f32[128,2048]{1,0:T(8,128)}, u32[]{:S(2)}) copy-start(f32[128,2048]{1,0:T(8,128)} %param.33) | copy-start | bytes 3145732
  1516.8 333.4 %copy-start.26 = (f32[128,2048]{1,0:T(8,128)S(1)}, f32[128,2048]{1,0:T(8,128)}, u32[]{:S(2)}) copy-start(f32[128,2048]{1,0:T(8,128)} %get-tuple-element.297) | copy-start | bytes 3145732
  1801.7 51.5 %copy-start.16 = (f32[256,1024]{1,0:T(8,128)S(1)}, f32[256,1024]{1,0:T(8,128)}, u32[]{:S(2)}) copy-start(f32[256,1024]{1,0:T(8,128)} %param.32) | copy-start | bytes 3145732
  1845.3 9.7 copy-start.53
  1845.3 8.0 copy-start.27
  1845.3 8.0 copy-start.28
  1850.2 4.8 copy-start.19
  1850.2 4.8 copy-start.29
  1850.2 4.8 copy-start.30
  (23 other events, 51.6 us)
Sparse Core Ops, SparseCore 0:
  10.8 75.4 all-gather.13
  88.4 32.9 all-gather.9
  124.2 124.4 all-gather.11
  251.3 70.9 all-gather.15
  331.4 69.9 reduce-scatter.9
  403.9 72.7 all-gather.19
  478.8 32.9 all-gather.17
  513.4 34.4 all-gather.23
  550.6 72.7 all-gather.21
  650.6 69.9 reduce-scatter.13
  725.9 34.4 all-gather.25
  764.5 147.4 reduce-scatter.25
  916.2 146.5 reduce-scatter.23
  1065.2 70.4 reduce-scatter.15
  1139.8 147.4 reduce-scatter.21
  1291.3 146.5 reduce-scatter.17
  1440.3 70.5 reduce-scatter.11
  1515.1 279.4 reduce-scatter.19
where the time goes:
time: 1880 us; the launch traced here: 1870 us
  waiting for transfers between devices  1370 us (73%)
  matrix products  213 us (11%)
  local copies, waits for them, and re-layouts  129 us (7%)
  other arithmetic  99.3 us (5%)
  blocking collectives  39.4 us (2%)
    reduce_scatter x1, waiting for transfers between devices, body(): lax.psum_scatter(mixing_local, 'dp', scatter_dimension=1, tiled=True)  278 us
    reduce_scatter x1, waiting for transfers between devices, body(): lax.psum_scatter(output_local, 'dp', scatter_dimension=0, tiled=True)  149 us
    reduce_scatter x1, waiting for transfers between devices, body(): lax.psum_scatter(scoring_local, 'dp', scatter_dimension=1, tiled=True)  146 us
    all_gather x1, waiting for transfers between devices, body(): lax.all_gather(mixing_master.astype(jnp.bfloat16), 'dp', axis=1, tiled=True)  113 us
    reduce_scatter x1, waiting for transfers between devices, body(): lax.psum_scatter(expand_local, 'dp', scatter_dimension=0, tiled=True)  98.1 us
    all_gather x1, waiting for transfers between devices, body(): lax.all_gather(shrink_master.astype(jnp.bfloat16), 'dp', axis=0, tiled=True)  75.5 us
    reduce_scatter x1, waiting for transfers between devices, body(): lax.psum_scatter(contract_cols(upward_back, expand_low), 'mp', scatter_di...  70.1 us
    all_gather x1, waiting for transfers between devices, body(): lax.all_gather(expand_master.astype(jnp.bfloat16), 'dp', axis=0, tiled=True)  68.9 us
  transfers between devices with their start and end apart: 18, of which 17 were waited for; matrix products, arithmetic and copies ran while one was open for 19% of the time, Pallas kernels for 0%

commit v1 on v0

--- a/solution.py
+++ b/solution.py
@@ -11,6 +11,19 @@
 decay_rate = 0.01
 learn_rate = 0.5
 norm_epsilon = 1e-06
+
+
+def gather_around(value, axis, dim):
+    peers, index, span = (lax.axis_size(axis), lax.axis_index(axis), value.shape[dim])
+    forward = [(i, (i + 1) % peers) for i in range(peers)]
+    whole = jnp.zeros((*value.shape[:dim], peers * span, *value.shape[dim + 1 :]), value.dtype)
+    held = value
+    for turn in range(peers):
+        holder = (index - turn) % peers
+        whole = lax.dynamic_update_slice_in_dim(whole, held, holder * span, axis=dim)
+        if turn < peers - 1:
+            held = lax.ppermute(held, axis, forward)
+    return whole
 
 
 def rms_scale(values, gain_row):
@@ -150,7 +163,7 @@
     shrink_second,
 ):
     scoring_low, mixing_low, output_low, expand_low, shrink_low = (
-        lax.all_gather(scoring_master.astype(jnp.bfloat16), "dp", axis=1, tiled=True),
+        gather_around(scoring_master.astype(jnp.bfloat16), "dp", 1),
         lax.all_gather(mixing_master.astype(jnp.bfloat16), "dp", axis=1, tiled=True),
         lax.all_gather(output_master.astype(jnp.bfloat16), "dp", axis=0, tiled=True),
         lax.all_gather(expand_master.astype(jnp.bfloat16), "dp", axis=0, tiled=True),

time: 1880 us -> 1840 us (0.979)
  waiting for transfers between devices: 1370 us -> 1320 us
    ppermute x0 -> x7, waiting for transfers between devices: none -> 125 us  [gather_around(): held = lax.ppermute(held, axis, forward)]
    all_gather x1, waiting for transfers between devices: 113 us -> 24.2 us  [body(): lax.all_gather(mixing_master.astype(jnp.bfloat16), 'dp', axis=1, tiled=True)]
    all_gather x1 -> x0, waiting for transfers between devices: 65.3 us -> none  [body(): lax.all_gather(scoring_master.astype(jnp.bfloat16), 'dp', axis=1, tiled=T...]
    all_gather x1, waiting for transfers between devices: 19.4 us -> 0.01 us  [body(): normed_all = lax.all_gather(normed, 'mp', axis=0, tiled=True)]
  transfers between devices with their start and end apart: 18 -> 24, of which waited for: 17 -> 22; matrix products, arithmetic and copies ran while one was open for 19% -> 20% of each run, Pallas kernels for 0% -> 0%
where the time goes in v1:
time: 1840 us; the launch traced here: 1830 us
  waiting for transfers between devices  1320 us (72%)
  matrix products  208 us (11%)
  local copies, waits for them, and re-layouts  142 us (8%)
  other arithmetic  99.1 us (5%)
  blocking collectives  39.4 us (2%)
    reduce_scatter x1, waiting for transfers between devices, body(): lax.psum_scatter(mixing_local, 'dp', scatter_dimension=1, tiled=True)  278 us
    reduce_scatter x1, waiting for transfers between devices, body(): lax.psum_scatter(output_local, 'dp', scatter_dimension=0, tiled=True)  149 us
    reduce_scatter x1, waiting for transfers between devices, body(): lax.psum_scatter(scoring_local, 'dp', scatter_dimension=1, tiled=True)  146 us
    ppermute x7, waiting for transfers between devices, gather_around(): held = lax.ppermute(held, axis, forward)  125 us
    reduce_scatter x1, waiting for transfers between devices, body(): lax.psum_scatter(expand_local, 'dp', scatter_dimension=0, tiled=True)  102 us
    all_gather x1, waiting for transfers between devices, body(): lax.all_gather(shrink_master.astype(jnp.bfloat16), 'dp', axis=0, tiled=True)  75.5 us
    reduce_scatter x1, waiting for transfers between devices, body(): lax.psum_scatter(contract_cols(upward_back, expand_low), 'mp', scatter_di...  70 us
    all_gather x1, waiting for transfers between devices, body(): lax.all_gather(expand_master.astype(jnp.bfloat16), 'dp', axis=0, tiled=True)  69 us
  transfers between devices with their start and end apart: 24, of which 22 were waited for; matrix products, arithmetic and copies ran while one was open for 20% of the time, Pallas kernels for 0%

profile of v1, /device:TPU:0, one launch (start us, length us, event | category | flops | bytes accessed | tf_op | source)
XLA Modules:
  0.0 1834.9 jit_solution(15550542532874936303)
XLA Ops:
  18.6 15.0 collective-permute-done
  33.5 15.8 collective-permute-done.1
  50.1 14.1 collective-permute-done.2
  64.3 27.3 %collective-permute-done.3 = bf16[2,256,512]{2,1,0:T(8,128)(2,1)S(1)} collective-permute-done((bf16[2,256,512]{2,1,0:T(8,128)(2,1)S(1)}, bf16[2,256,512]{2,1,0:T(8,128)(2,1)S(1)}, u32[]{:S(2)}, u32[]{:S(2)}) %collective-permute-start.3) | collective-permute-done | bytes 524320 | tf_op jit(solution)/shard_map/ppermute | solution.py:25
  92.5 26.2 %collective-permute-done.4 = bf16[2,256,512]{2,1,0:T(8,128)(2,1)} collective-permute-done((bf16[2,256,512]{2,1,0:T(8,128)(2,1)S(1)}, bf16[2,256,512]{2,1,0:T(8,128)(2,1)}, u32[]{:S(2)}, u32[]{:S(2)}) %collective-permute-start.4) | collective-permute-done | bytes 524320 | tf_op jit(solution)/shard_map/ppermute | solution.py:25
  129.2 6.5 collective-permute-done.5
  143.2 20.4 %collective-permute-done.6 = bf16[2,256,512]{2,1,0:T(8,128)(2,1)S(1)} collective-permute-done((bf16[2,256,512]{2,1,0:T(8,128)(2,1)}, bf16[2,256,512]{2,1,0:T(8,128)(2,1)S(1)}, u32[]{:S(2)}, u32[]{:S(2)}) %collective-permute-start.6) | collective-permute-done | bytes 524320 | tf_op jit(solution)/shard_map/ppermute | solution.py:25
  168.7 4.4 dot_general.103
  175.7 5.4 fusion.20
  190.1 24.2 %all-gather.11.cloned.1.call-done = bf16[2,2048,1024]{2,1,0:T(8,128)(2,1)} async-done(((bf16[2,256,1024]{2,1,0:T(8,128)(2,1)}), bf16[2,2048,1024]{2,1,0:T(8,128)(2,1)}) %all-gather.11.cloned.1.call-update) | async-done | bytes 8388624 | tf_op jit(solution)/shard_map/all_gather | solution.py:167
  214.3 8.0 fusion.51
  224.9 4.6 slice_bitcast_fusion.3
  229.5 6.5 copy.92
  236.0 18.2 while.26
  239.5 5.4 bitcast_dynamic-update-slice_fusion.2
  248.3 5.9 bitcast_dynamic-update-slice_fusion.2
  254.2 7.3 copy.108
  261.5 7.0 reshape.309
  272.1 10.5 multiply_convert_fusion.4
  282.5 6.3 all-gather.13.cloned.1.call-done
  288.8 8.9 fusion.83
  299.9 68.0 %reduce-scatter.10.cloned.1.call-done = f32[256,2048]{1,0:T(8,128)} async-done(((f32[1024,2048]{1,0:T(8,128)}), f32[256,2048]{1,0:T(8,128)}) %reduce-scatter.10.cloned.1.call-update) | async-done | bytes 2097168 | tf_op jit(solution)/shard_map/reduce_scatter | solution.py:206
  374.2 69.0 %all-gather.17.cloned.1.call-done = bf16[2048,1024]{1,0:T(8,128)(2,1)} async-done(((bf16[256,1024]{1,0:T(8,128)(2,1)}), bf16[2048,1024]{1,0:T(8,128)(2,1)}) %all-gather.17.cloned.1.call-update) | async-done | bytes 4194320 | tf_op jit(solution)/shard_map/all_gather | solution.py:169
  443.2 35.0 %all-gather.15.cloned.1.call-done = bf16[1024,2048]{1,0:T(8,128)(2,1)} async-done(((bf16[256,2048]{1,0:T(8,128)(2,1)}), bf16[1024,2048]{1,0:T(8,128)(2,1)}) %all-gather.15.cloned.1.call-update) | async-done | bytes 4194320 | tf_op jit(solution)/shard_map/all_gather | solution.py:214
  478.2 10.1 fusion.84
  488.3 26.0 %all-gather.21.cloned.1.call-done = bf16[1024,2048]{1,0:T(8,128)(2,1)} async-done(((bf16[256,2048]{1,0:T(8,128)(2,1)}), bf16[1024,2048]{1,0:T(8,128)(2,1)}) %all-gather.21.cloned.1.call-update) | async-done | bytes 4194320 | tf_op jit(solution)/shard_map/all_gather | solution.py:224
  514.3 75.5 %all-gather.19.cloned.1.call-done = bf16[1024,2048]{1,0:T(8,128)(2,1)} async-done(((bf16[128,2048]{1,0:T(8,128)(2,1)}), bf16[1024,2048]{1,0:T(8,128)(2,1)}) %all-gather.19.cloned.1.call-update) | async-done | bytes 4194320 | tf_op jit(solution)/shard_map/all_gather | solution.py:170
  589.8 18.9 %add_convert_fusion = (bf16[1024,1024]{1,0:T(8,128)(2,1)S(1)}, f32[1024,1024]{1,0:T(8,128)}) fusion(f32[1024,1024]{1,0:T(8,128)} %fusion.84, bf16[1024,2048]{1,0:T(8,128)(2,1)} %all-gather.21.cloned.1.call-done, bf16[1024,2048]{1,0:T(8,128)(2,1)} %all-gather.19.cloned.1.call-done), kind=kOutput, calls=%fused_computation.54 | convolution fusion | flops 4370464768 | bytes 18874368 | tf_op jit(solution)/shard_map/dot_general | solution.py:78
  610.0 6.9 fusion.86
  616.9 70.0 %reduce-scatter.14.cloned.1.call-done = f32[256,2048]{1,0:T(8,128)} async-done(((f32[1024,2048]{1,0:T(8,128)}), f32[256,2048]{1,0:T(8,128)}) %reduce-scatter.14.cloned.1.call-update) | async-done | bytes 2097168 | tf_op jit(solution)/shard_map/reduce_scatter | solution.py:230
  692.2 4.7 multiply_convert_fusion.3
  698.3 7.2 fusion.89
  707.0 9.1 fusion.88
  716.2 10.6 all-gather.23.cloned.1.call-done
  726.7 11.1 multiply_reduce_fusion
  737.9 4.5 fusion.16
  742.4 81.4 %while.27 = (s32[]{:T(128)}, f32[1024,2,256]{0,2,1:T(8,128)}, f32[1024,2,512]{0,2,1:T(8,128)}, f32[2,512,2,256]{1,0,3,2:T(2,128)}, s32[2]{0:T(128)S(1)}, /*index...) while((s32[]{:T(128)}, f32[1024,2,256]{0,2,1:T(8,128)}, ...), condition=%wide.region_11.13_spmd.clone, body=%wide.region_10.12_spmd.clone.sunk | while | flops 3772776960 | bytes 48765212 | solution.py:130
  745.8 4.6 multiply_convert_fusion.7
  755.2 6.8 bitcast_add_fusion.5
  762.0 19.6 %dynamic_update_slice.54 = f32[2,512,2,256]{1,0,3,2:T(2,128)} dynamic-update-slice(f32[2,512,2,256]{1,0,3,2:T(2,128)} %get-tuple-element.510, f32[1,512,2,256]{1,0,3,2:T(1,128)S(1)} %copy.180, s32[]{:T(128)S(6)} %copy.201, s32[]{:T(128)} %constant.93.clone.1..sunk.1, s32[]{:T(128)} %constant.93.clone.1..sunk.1, s32[]{:T(128)} %constant.93.clone.1..sunk.1) | dynamic-update-slice | bytes 2097156 | tf_op jit(solution)/shard_map/while/body/jit(dynamic_update_index_in_dim)/dynamic_update_slice | solution.py:130
  785.1 4.6 multiply_convert_fusion.7
  796.1 8.0 bitcast_add_fusion.5
  804.2 19.6 %dynamic_update_slice.54 = f32[2,512,2,256]{1,0,3,2:T(2,128)} dynamic-update-slice(f32[2,512,2,256]{1,0,3,2:T(2,128)} %get-tuple-element.510, f32[1,512,2,256]{1,0,3,2:T(1,128)S(1)} %copy.180, s32[]{:T(128)S(6)} %copy.201, s32[]{:T(128)} %constant.93.clone.1..sunk.1, s32[]{:T(128)} %constant.93.clone.1..sunk.1, s32[]{:T(128)} %constant.93.clone.1..sunk.1) | dynamic-update-slice | bytes 2097156 | tf_op jit(solution)/shard_map/while/body/jit(dynamic_update_index_in_dim)/dynamic_update_slice | solution.py:130
  842.1 4.8 fusion.46
  847.0 4.6 fusion.24
  851.6 6.8 fusion.34
  858.4 11.0 add_add_fusion
  871.1 9.0 fusion.87
  881.3 4.8 convolution_bitcast_fusion.3
  894.5 8.8 fusion.85
  903.4 7.2 convolution_bitcast_fusion.2
  910.6 4.7 convolution_bitcast_fusion.1
  915.3 6.3 pad_maximum_fusion
  927.5 101.6 %reduce-scatter.24.cloned.1.call-done = f32[256,1024]{1,0:T(8,128)} async-done(((f32[2048,1024]{1,0:T(8,128)}), f32[256,1024]{1,0:T(8,128)}) %reduce-scatter.24.cloned.1.call-update) | async-done | bytes 1048592 | tf_op jit(solution)/shard_map/reduce_scatter | solution.py:271
  1029.1 4.5 multiply_reduce_fusion.12
  1033.6 68.6 %reduce-scatter.16.cloned.1.call-done = f32[256,2048]{1,0:T(8,128)} async-done(((f32[1024,2048]{1,0:T(8,128)}), f32[256,2048]{1,0:T(8,128)}) %reduce-scatter.16.cloned.1.call-update) | async-done | bytes 2097168 | tf_op jit(solution)/shard_map/reduce_scatter | solution.py:261
  1104.5 149.2 %reduce-scatter.22.cloned.1.call-done = f32[128,2048]{1,0:T(8,128)} async-done(((f32[1024,2048]{1,0:T(8,128)}), f32[128,2048]{1,0:T(8,128)}) %reduce-scatter.22.cloned.1.call-update) | async-done | bytes 1048592 | tf_op jit(solution)/shard_map/reduce_scatter | solution.py:270
  1253.7 4.5 multiply_reduce_fusion.13
  1258.3 146.1 %reduce-scatter.18.cloned.1.call-done = f32[2,256,512]{2,1,0:T(8,128)} async-done(((f32[2,2048,512]{2,1,0:T(8,128)}), f32[2,256,512]{2,1,0:T(8,128)}) %reduce-scatter.18.cloned.1.call-update) | async-done | bytes 1048592 | tf_op jit(solution)/shard_map/reduce_scatter | solution.py:268
  1408.7 68.7 %reduce-scatter.12.cloned.1.call-done = f32[256,2048]{1,0:T(8,128)} async-done(((f32[1024,2048]{1,0:T(8,128)}), f32[256,2048]{1,0:T(8,128)}) %reduce-scatter.12.cloned.1.call-update) | async-done | bytes 2097168 | tf_op jit(solution)/shard_map/reduce_scatter | solution.py:217
  1477.4 5.9 fusion.42
  1483.3 277.8 %reduce-scatter.20.cloned.1.call-done = f32[2,256,1024]{2,1,0:T(8,128)} async-done(((f32[2,2048,1024]{2,1,0:T(8,128)}), f32[2,256,1024]{2,1,0:T(8,128)}) %reduce-scatter.20.cloned.1.call-update) | async-done | bytes 2097168 | tf_op jit(solution)/shard_map/reduce_scatter | solution.py:269
  1761.1 7.1 multiply_reduce_fusion.3
  1772.4 39.4 %all-reduce = (f32[2,2048]{1,0:T(2,128)S(1)}, f32[7]{0:T(128)S(1)}, f32[7]{0:T(128)S(1)}) all-reduce(f32[2,2048]{1,0:T(2,128)S(1)} %pad_maximum_fusion.4, f32[7]{0:T(128)S(1)} %concatenate.16, f32[7]{0:T(128)S(1)} %concatenate.15), channel_id=1, replica_groups=mesh['dp'=8,'mp'=4] {'dp','mp'}, use_global_device_ids=true, to_apply=%region_16.18 | all-reduce | flops 4110 | bytes 32880 | tf_op jit(solution)/shard_map/psum | solution.py:274
  (309 shorter events, 153.7 us)
Async XLA Ops:
  7.2 5.8 copy-start.5
  7.2 168.5 %all-gather.9.cloned.1.call-start = ((), (), s32[]{:S(2)}) async-start(), calls=%async_computation.9 | async-start | bytes 5242880 | tf_op jit(solution)/shard_map/all_gather | solution.py:187
  9.8 680.0 %copy-start.44 = (f32[1,2048]{1,0:T(1,128)}, f32[1,2048]{1,0:T(1,128)S(1)}, u32[]{:S(2)}) copy-start(f32[1,2048]{1,0:T(1,128)S(1)} %get-tuple-element.334) | copy-start | bytes 24580
  10.4 81.2 %copy-start.16 = (f32[128,2048]{1,0:T(8,128)S(1)}, f32[128,2048]{1,0:T(8,128)}, u32[]{:S(2)}) copy-start(f32[128,2048]{1,0:T(8,128)} %param.31) | copy-start | bytes 3145732
  13.0 201.4 %all-gather.11.cloned.1.call-start = ((), (), s32[]{:S(2)}) async-start(), calls=%async_computation.10 | async-start | bytes 9437184 | tf_op jit(solution)/shard_map/all_gather | solution.py:167
  14.2 274.6 %all-gather.13.cloned.1.call-start = ((), (), s32[]{:S(2)}) async-start(), calls=%async_computation.11 | async-start | bytes 4718592 | tf_op jit(solution)/shard_map/all_gather | solution.py:168
  15.5 18.0 collective-permute-start
  33.5 85.4 %copy-start.42 = (bf16[2,256,512]{2,1,0:T(8,128)(2,1)}, bf16[2,256,512]{2,1,0:T(8,128)(2,1)S(1)}, u32[]{:S(2)}) copy-start(bf16[2,256,512]{2,1,0:T(8,128)(2,1)S(1)} %collective-permute-done) | copy-start | bytes 1572868
  33.5 15.8 collective-permute-start.1
  49.3 14.9 collective-permute-start.2
  64.2 27.3 %collective-permute-start.3 = (bf16[2,256,512]{2,1,0:T(8,128)(2,1)S(1)}, bf16[2,256,512]{2,1,0:T(8,128)(2,1)S(1)}, u32[]{:S(2)}, u32[]{:S(2)}) collective-permute-start(bf16[2,256,512]{2,1,0:T(8,128)(2,1)S(1)} %collective-permute-done.2), channel_id=1, source_target_pairs={{0,4},{4,8},{8,12},{12,16},{16,20},{20,24},{24,28},{28,0},{1,5},{5... | collective-permute-start | bytes 1572872 | tf_op jit(solution)/shard_map/ppermute | solution.py:25
  91.6 27.2 %collective-permute-start.4 = (bf16[2,256,512]{2,1,0:T(8,128)(2,1)S(1)}, bf16[2,256,512]{2,1,0:T(8,128)(2,1)}, u32[]{:S(2)}, u32[]{:S(2)}) collective-permute-start(bf16[2,256,512]{2,1,0:T(8,128)(2,1)S(1)} %collective-permute-done.3), channel_id=1, source_target_pairs={{0,4},{4,8},{8,12},{12,16},{16,20},{20,24},{24,28},{28,0},{1,5},{5... | collective-permute-start | bytes 1572872 | tf_op jit(solution)/shard_map/ppermute | solution.py:25
  92.5 275.4 %reduce-scatter.10.cloned.1.call-start = ((), (), s32[]{:S(2)}) async-start(), calls=%async_computation.12 | async-start | bytes 10485760 | tf_op jit(solution)/shard_map/reduce_scatter | solution.py:206
  118.8 17.0 collective-permute-start.5
  125.6 58.0 %copy-start.22 = (f32[1024,128]{0,1:T(8,128)}, f32[1024,128]{0,1:T(8,128)S(1)}, u32[]{:S(2)}) copy-start(f32[1024,128]{0,1:T(8,128)S(1)} %get-tuple-element.349) | copy-start | bytes 1572868
  135.7 27.9 %collective-permute-start.6 = (bf16[2,256,512]{2,1,0:T(8,128)(2,1)}, bf16[2,256,512]{2,1,0:T(8,128)(2,1)S(1)}, u32[]{:S(2)}, u32[]{:S(2)}) collective-permute-start(bf16[2,256,512]{2,1,0:T(8,128)(2,1)} %collective-permute-done.5), channel_id=1, source_target_pairs={{0,4},{4,8},{8,12},{12,16},{16,20},{20,24},{24,28},{28,0},{1,5},{5... | collective-permute-start | bytes 1572872 | tf_op jit(solution)/shard_map/ppermute | solution.py:25
  175.7 5.4 copy-start.61
  282.5 15.2 copy-start.66
  297.7 70.1 %copy-start.3 = (bf16[256,2048]{1,0:T(8,128)(2,1)S(1)}, bf16[256,2048]{1,0:T(8,128)(2,1)}, u32[]{:S(2)}) copy-start(bf16[256,2048]{1,0:T(8,128)(2,1)} %param.26) | copy-start | bytes 3145732
  297.8 145.5 %all-gather.17.cloned.1.call-start = ((), (), s32[]{:S(2)}) async-start(), calls=%async_computation.14 | async-start | bytes 4718592 | tf_op jit(solution)/shard_map/all_gather | solution.py:169
  299.9 178.4 %all-gather.15.cloned.1.call-start = ((), (), s32[]{:S(2)}) async-start(), calls=%async_computation.13 | async-start | bytes 5242880 | tf_op jit(solution)/shard_map/all_gather | solution.py:214
  369.8 320.0 %copy-start = (f32[256,2048]{1,0:T(8,128)}, f32[256,2048]{1,0:T(8,128)S(1)}, u32[]{:S(2)}) copy-start(f32[256,2048]{1,0:T(8,128)S(1)} %get-tuple-element.310) | copy-start | bytes 6291460
  369.8 320.0 %copy-start.50 = (f32[256]{0:T(256)}, f32[256]{0:T(256)S(1)}, u32[]{:S(2)}) copy-start(f32[256]{0:T(256)S(1)} %fusion.62) | copy-start | bytes 3076
  371.3 143.0 %all-gather.21.cloned.1.call-start = ((), (), s32[]{:S(2)}) async-start(), calls=%async_computation.17 | async-start | bytes 5242880 | tf_op jit(solution)/shard_map/all_gather | solution.py:224
  372.0 217.8 %all-gather.19.cloned.1.call-start = ((), (), s32[]{:S(2)}) async-start(), calls=%async_computation.15 | async-start | bytes 4718592 | tf_op jit(solution)/shard_map/all_gather | solution.py:170
  374.2 312.8 %reduce-scatter.14.cloned.1.call-start = ((), (), s32[]{:S(2)}) async-start(), calls=%async_computation.18 | async-start | bytes 10485760 | tf_op jit(solution)/shard_map/reduce_scatter | solution.py:230
  589.8 20.2 %copy-start.65 = (bf16[2048,1024]{1,0:T(8,128)(2,1)S(1)}, bf16[2048,1024]{1,0:T(8,128)(2,1)}, u32[]{:S(2)}) copy-start(bf16[2048,1024]{1,0:T(8,128)(2,1)} %all-gather.17.cloned.1.call-done) | copy-start | bytes 12582916
  616.9 73.5 %copy-start.10 = (bf16[256,2048]{1,0:T(8,128)(2,1)S(1)}, bf16[256,2048]{1,0:T(8,128)(2,1)}, u32[]{:S(2)}) copy-start(bf16[256,2048]{1,0:T(8,128)(2,1)} %param.27) | copy-start | bytes 3145732
  616.9 109.9 %all-gather.23.cloned.1.call-start = ((), (), s32[]{:S(2)}) async-start(), calls=%async_computation.19 | async-start | bytes 5242880 | tf_op jit(solution)/shard_map/all_gather | solution.py:237
  692.1 229.6 %reduce-scatter.26.cloned.1.call-start = ((), (), s32[]{:S(2)}) async-start(), calls=%async_computation.25 | async-start | bytes 9437184 | tf_op jit(solution)/shard_map/reduce_scatter | solution.py:272
  692.2 6.1 copy-start.64
  705.5 323.6 %reduce-scatter.24.cloned.1.call-start = ((), (), s32[]{:S(2)}) async-start(), calls=%async_computation.24 | async-start | bytes 9437184 | tf_op jit(solution)/shard_map/reduce_scatter | solution.py:271
  716.1 386.1 %reduce-scatter.16.cloned.1.call-start = ((), (), s32[]{:S(2)}) async-start(), calls=%async_computation.20 | async-start | bytes 10485760 | tf_op jit(solution)/shard_map/reduce_scatter | solution.py:261
  726.7 11.2 copy-start.9
  726.7 11.2 copy-start.24
  838.5 8.5 copy-start.39
  838.5 8.5 slice-start
  842.1 9.5 copy-start.37
  869.5 384.3 %reduce-scatter.22.cloned.1.call-start = ((), (), s32[]{:S(2)}) async-start(), calls=%async_computation.23 | async-start | bytes 9437184 | tf_op jit(solution)/shard_map/reduce_scatter | solution.py:270
  880.1 524.3 %reduce-scatter.18.cloned.1.call-start = ((), (), s32[]{:S(2)}) async-start(), calls=%async_computation.21 | async-start | bytes 9437184 | tf_op jit(solution)/shard_map/reduce_scatter | solution.py:268
  892.9 584.5 %reduce-scatter.12.cloned.1.call-start = ((), (), s32[]{:S(2)}) async-start(), calls=%async_computation.16 | async-start | bytes 10485760 | tf_op jit(solution)/shard_map/reduce_scatter | solution.py:217
  903.3 7.3 copy-start.36
  903.3 857.8 %reduce-scatter.20.cloned.1.call-start = ((), (), s32[]{:S(2)}) async-start(), calls=%async_computation.22 | async-start | bytes 18874368 | tf_op jit(solution)/shard_map/reduce_scatter | solution.py:269
  903.4 7.2 copy-start.63
  921.7 107.4 %copy-start.14 = (f32[256,1024]{1,0:T(8,128)S(1)}, f32[256,1024]{1,0:T(8,128)}, u32[]{:S(2)}) copy-start(f32[256,1024]{1,0:T(8,128)} %param.32) | copy-start | bytes 3145732
  927.5 174.8 %copy-start.4 = (bf16[256,2048]{1,0:T(8,128)(2,1)S(1)}, bf16[256,2048]{1,0:T(8,128)(2,1)}, u32[]{:S(2)}) copy-start(bf16[256,2048]{1,0:T(8,128)(2,1)} %param.26) | copy-start | bytes 3145732
  927.5 174.8 %copy-start.48 = (f32[1,2048]{1,0:T(1,128)S(1)}, f32[1,2048]{1,0:T(1,128)}, u32[]{:S(2)}) copy-start(f32[1,2048]{1,0:T(1,128)} %copy-done.47) | copy-start | bytes 24580
  927.5 174.8 %copy-start.53 = (f32[256]{0:T(256)S(1)}, f32[256]{0:T(256)}, u32[]{:S(2)}) copy-start(f32[256]{0:T(256)} %copy-done.52) | copy-start | bytes 3076
  927.5 177.0 %copy-start.60 = (f32[256]{0:T(256)S(1)}, f32[256]{0:T(256)}, u32[]{:S(2)}) copy-start(f32[256]{0:T(256)} %copy-done.59) | copy-start | bytes 3076
  927.5 177.1 %copy-start.49 = (f32[2048]{0:T(1024)S(1)}, f32[2048]{0:T(1024)}, u32[]{:S(2)}) copy-start(f32[2048]{0:T(1024)} %get-tuple-element.232) | copy-start | bytes 24580
  927.5 326.3 %copy-start.17 = (f32[128,2048]{1,0:T(8,128)S(1)}, f32[128,2048]{1,0:T(8,128)}, u32[]{:S(2)}) copy-start(f32[128,2048]{1,0:T(8,128)} %param.31) | copy-start | bytes 3145732
  1258.3 219.1 %copy-start.1 = (f32[256,2048]{1,0:T(8,128)S(1)}, f32[256,2048]{1,0:T(8,128)}, u32[]{:S(2)}) copy-start(f32[256,2048]{1,0:T(8,128)} %copy-done) | copy-start | bytes 6291460
  1258.3 219.1 %copy-start.45 = (f32[1,2048]{1,0:T(1,128)S(1)}, f32[1,2048]{1,0:T(1,128)}, u32[]{:S(2)}) copy-start(f32[1,2048]{1,0:T(1,128)} %copy-done.44) | copy-start | bytes 24580
  1258.3 219.1 %copy-start.51 = (f32[256]{0:T(256)S(1)}, f32[256]{0:T(256)}, u32[]{:S(2)}) copy-start(f32[256]{0:T(256)} %copy-done.50) | copy-start | bytes 3076
  1258.3 219.1 %copy-start.58 = (f32[256]{0:T(256)S(1)}, f32[256]{0:T(256)}, u32[]{:S(2)}) copy-start(f32[256]{0:T(256)} %copy-done.57) | copy-start | bytes 3076
  1483.3 331.2 %copy-start.46 = (f32[2,2048]{1,0:T(2,128)S(1)}, f32[2,2048]{1,0:T(2,128)}, u32[]{:S(2)}) copy-start(f32[2,2048]{1,0:T(2,128)} %param.28) | copy-start | bytes 49156
  1483.3 331.2 %copy-start.54 = (f32[2,2048]{1,0:T(2,128)S(1)}, f32[2,2048]{1,0:T(2,128)}, u32[]{:S(2)}) copy-start(f32[2,2048]{1,0:T(2,128)} %param.35) | copy-start | bytes 49156
  1483.3 331.2 %copy-start.55 = (f32[2,2048]{1,0:T(2,128)S(1)}, f32[2,2048]{1,0:T(2,128)}, u32[]{:S(2)}) copy-start(f32[2,2048]{1,0:T(2,128)} %param.34) | copy-start | bytes 49156
  1483.3 333.4 %copy-start.12 = (f32[128,2048]{1,0:T(8,128)S(1)}, f32[128,2048]{1,0:T(8,128)}, u32[]{:S(2)}) copy-start(f32[128,2048]{1,0:T(8,128)} %param.33) | copy-start | bytes 3145732
  1483.3 333.4 %copy-start.25 = (f32[128,2048]{1,0:T(8,128)S(1)}, f32[128,2048]{1,0:T(8,128)}, u32[]{:S(2)}) copy-start(f32[128,2048]{1,0:T(8,128)} %get-tuple-element.297) | copy-start | bytes 3145732
  1768.3 51.5 %copy-start.15 = (f32[256,1024]{1,0:T(8,128)S(1)}, f32[256,1024]{1,0:T(8,128)}, u32[]{:S(2)}) copy-start(f32[256,1024]{1,0:T(8,128)} %param.32) | copy-start | bytes 3145732
  1811.8 9.7 copy-start.56
  1811.8 8.0 copy-start.26
  1811.8 8.0 copy-start.27
  (33 other events, 92.4 us)
Sparse Core Ops, SparseCore 0:
  13.1 37.1 all-gather.8
  53.1 161.2 all-gather.10
  217.0 71.7 all-gather.12
  297.9 69.9 reduce-scatter.9
  370.4 72.7 all-gather.16
  445.2 32.9 all-gather.14
  479.8 34.4 all-gather.20
  517.0 72.7 all-gather.18
  617.0 69.9 reduce-scatter.13
  692.2 34.4 all-gather.22
  730.9 147.4 reduce-scatter.25
  882.5 146.5 reduce-scatter.23
  1031.6 70.5 reduce-scatter.15
  1106.3 147.4 reduce-scatter.21
  1257.8 146.5 reduce-scatter.17
  1406.8 70.4 reduce-scatter.11
  1481.5 279.5 reduce-scatter.19
